TPU v7x, 32 devices: a whole 2x2x4 slice. The times are simulated.
32 devices in a mesh: groups: 2 (over y), tensor: 4 (over z), dp: 4 (over x, core).
Axes of the slice: x: 2, y: 2, z: 4, core: 2. Of those that a mesh axis runs over, the one named last changes fastest.
Arguments:
- out_grad: bfloat16 [4, 1280, 4096], P('dp', ('groups', 'tensor')), parts along dimension 1, may hold values from -6 to 6
- gate_pre: bfloat16 [4, 1280, 14336], P('dp', 'groups', 'tensor'), parts along dimension 1, may hold values from -8 to 8
- up_pre: bfloat16 [4, 1280, 14336], P('dp', 'groups', 'tensor'), parts along dimension 1, may hold values from -6 to 6
- down_weight: bfloat16 [14336, 4096], P('tensor'), may hold values from -0.046875 to 0.046875
Outputs:
- gate_grad: bfloat16 [4, 1280, 14336], P('dp', 'groups', 'tensor'), parts along dimension 1
- up_grad: bfloat16 [4, 1280, 14336], P('dp', 'groups', 'tensor'), parts along dimension 1
- down_grad: bfloat16 [28672, 4096], P(('groups', 'tensor'), 'dp'), parts along dimension 0
There are 2 independent parts, one for each index of `groups`. A program takes and returns all parts, laid end to end along the dimension named above; an argument that names none is the same for every part. Nothing has to cross between parts.
All inputs are finite; a program needn't handle non-finite values.
Results may differ from a plain program's by a relative error of at most 0.014.
Values may be sent and summed in bfloat16 or wider, within the bound.
A program may use at most 128 MiB of HBM per device.

v0:
```python
import math

import jax
import jax.numpy as jnp
from jax import lax
from jax.sharding import PartitionSpec as P


def times_down(block, down_weight):
    return lax.dot_general(
        block, down_weight, (((1,), (1,)), ((), ())), preferred_element_type=jnp.float32
    )


def on_device(out_grad, gate_pre, up_pre, down_weight):
    gate = gate_pre[0].astype(jnp.float32)
    up = up_pre[0].astype(jnp.float32)
    sig = jax.nn.sigmoid(gate)
    act = gate * sig
    hidden = (act * up).astype(jnp.bfloat16)
    group_rows = hidden.shape[0]
    scale = 1.0 / math.sqrt(group_rows * lax.axis_size("dp"))
    block = lax.all_gather(out_grad, "tensor", axis=1, tiled=True)[0]
    weight_acc = jnp.einsum("tf,td->fd", hidden, block, preferred_element_type=jnp.float32)
    hidden_grad = times_down(block, down_weight)
    weight_acc, hidden_grad = (weight_acc, hidden_grad)
    down_grad = lax.psum_scatter(
        (weight_acc * scale).astype(jnp.bfloat16), "dp", scatter_dimension=1, tiled=True
    )
    gate_grad = (hidden_grad * up * sig * (1.0 + gate * (1.0 - sig))).astype(jnp.bfloat16)
    up_grad = (hidden_grad * act).astype(jnp.bfloat16)
    return (gate_grad[None], up_grad[None], down_grad)


def solution(mesh):
    return jax.shard_map(
        on_device,
        mesh=mesh,
        in_specs=(
            P("dp", ("groups", "tensor"), None),
            P("dp", "groups", "tensor"),
            P("dp", "groups", "tensor"),
            P("tensor", None),
        ),
        out_specs=(
            P("dp", "groups", "tensor"),
            P("dp", "groups", "tensor"),
            P(("groups", "tensor"), "dp"),
        ),
        check_vma=False,
    )
```

profile of v0, /device:TPU:13, one launch (start us, length us, event | category | flops | bytes accessed | tf_op | source)
XLA Modules:
  0.0 357.9 jit_solution(4585248660754477539)
XLA Ops:
  7.2 0.0 all-gather.2.cloned.1.call-start
  7.2 0.7 all-gather.2.cloned.1.call-update
  7.9 0.0 reduce-scatter.2.cloned.1.call-start
  7.9 98.2 %all-gather.2.cloned.1.call-done = bf16[1,640,4096]{2,1,0:T(8,128)(2,1)} async-done(((bf16[1,160,4096]{2,1,0:T(8,128)(2,1)}), bf16[1,640,4096]{2,1,0:T(8,128)(2,1)}) %all-gather.2.cloned.1.call-update) | async-done | bytes 5242896 | tf_op jit(solution)/shard_map/all_gather | solution.py:23
  106.2 35.9 %multiply_convert_fusion = bf16[3584,4096]{1,0:T(8,128)(2,1)} fusion(bf16[1,640,4096]{2,1,0:T(8,128)(2,1)} %all-gather.2.cloned.1.call-done, bf16[1,640,3584]{2,1,0:T(8,128)(2,1)} %param.6, bf16[1,640,3584]{2,1,0:T(8,128)(2,1)} %param.5), kind=kOutput, calls=%fused_computation | convolution fusion | flops 18838192128 | bytes 43778048 | tf_op jit(solution)/shard_map/tf,td->fd/dot_general | solution.py:24
  142.1 0.0 reduce-scatter.2.cloned.1.call-update
  142.1 32.8 %fusion.22 = (bf16[1,640,3584]{2,1,0:T(8,128)(2,1)}, bf16[1,640,3584]{2,1,0:T(8,128)(2,1)}) fusion(bf16[1,640,3584]{2,1,0:T(8,128)(2,1)} %param.5, bf16[1,640,3584]{2,1,0:T(8,128)(2,1)} %param.6, bf16[3584,4096]{1,0:T(8,128)(2,1)} %param.7, bf16[1,640,4096]{2,1,0:T(8,128)(2,1)} %all-gather.2.cloned.1.call-done), kind=kOutput, calls=%fused_computation.27 | convolution fusion | flops 18824888320 | bytes 52953088 | tf_op jit(solution)/shard_map/dot_general | solution.py:10
  174.9 176.2 %reduce-scatter.2.cloned.1.call-done = bf16[3584,1024]{1,0:T(8,128)(2,1)} async-done(((bf16[3584,4096]{1,0:T(8,128)(2,1)}), bf16[3584,1024]{1,0:T(8,128)(2,1)}) %reduce-scatter.2.cloned.1.call-update) | async-done | bytes 7340048 | tf_op jit(solution)/shard_map/reduce_scatter | solution.py:27
Async XLA Ops:
  7.2 99.0 %all-gather.2.cloned.1.call-start = ((), (), s32[]{:S(2)}) async-start(), calls=%async_computation.1 | async-start | bytes 6553600 | tf_op jit(solution)/shard_map/all_gather | solution.py:23
  7.9 343.2 %reduce-scatter.2.cloned.1.call-start = ((), (), s32[]{:S(2)}) async-start(), calls=%async_computation.2 | async-start | bytes 36700160 | tf_op jit(solution)/shard_map/reduce_scatter | solution.py:27
Sparse Core Ops, SparseCore 0:
  9.6 96.5 all-gather.1
  142.2 208.8 reduce-scatter.1
where the time goes:
time: 360 us; the launch traced here: 358 us
  waiting for transfers between devices  275 us (76%)
  matrix products  68.7 us (19%)
  between operations  14 us (4%)
    reduce_scatter x1, waiting for transfers between devices, on_device(): lax.psum_scatter((weight_acc * scale).astype(jnp.bfloat16), 'dp', scatter...  176 us
    all_gather x1, waiting for transfers between devices, on_device(): block = lax.all_gather(out_grad, 'tensor', axis=1, tiled=True)[0]  98.2 us
    dot_general x1, matrix products, on_device(): jnp.einsum('tf,td->fd', hidden, block, preferred_element_type=jnp.float32)  35.9 us
    dot_general x1, matrix products, times_down(): lax.dot_general(block, down_weight, (((1,), (1,)), ((), ())), preferred_e...  32.8 us
  transfers between devices with their start and end apart: 2, of which 2 were waited for; matrix products, arithmetic and copies ran while one was open for 9% of the time, Pallas kernels for 0%

commit v1 on v0

v1 whole, which is shorter than its diff:
```python
import math

import jax
import jax.numpy as jnp
from jax import lax
from jax.sharding import PartitionSpec as P


def on_device(out_grad, gate_pre, up_pre, down_weight):
    gate = gate_pre[0].astype(jnp.float32)
    up = up_pre[0].astype(jnp.float32)
    sig = jax.nn.sigmoid(gate)
    act = gate * sig
    hidden = (act * up).astype(jnp.bfloat16)
    scale = 1.0 / math.sqrt(hidden.shape[0] * lax.axis_size("dp"))
    hidden_all = lax.all_gather(hidden, "dp", axis=0, tiled=True)
    block = lax.all_gather(out_grad, "tensor", axis=1, tiled=True)[0]
    columns = lax.all_to_all(block, "dp", split_axis=1, concat_axis=0, tiled=True)
    hidden_grad = lax.dot_general(
        block, down_weight, (((1,), (1,)), ((), ())), preferred_element_type=jnp.float32
    )
    gate_grad = (hidden_grad * up * sig * (1.0 + gate * (1.0 - sig))).astype(jnp.bfloat16)
    up_grad = (hidden_grad * act).astype(jnp.bfloat16)
    total = jnp.einsum("tf,td->fd", hidden_all, columns, preferred_element_type=jnp.float32)
    down_grad = (total * scale).astype(jnp.bfloat16)
    return (gate_grad[None], up_grad[None], down_grad)


def solution(mesh):
    return jax.shard_map(
        on_device,
        mesh=mesh,
        in_specs=(
            P("dp", ("groups", "tensor"), None),
            P("dp", "groups", "tensor"),
            P("dp", "groups", "tensor"),
            P("tensor", None),
        ),
        out_specs=(
            P("dp", "groups", "tensor"),
            P("dp", "groups", "tensor"),
            P(("groups", "tensor"), "dp"),
        ),
        check_vma=False,
    )
```

time: 360 us -> 348 us (0.967)
  waiting for transfers between devices: 275 us -> 136 us
  blocking collectives: 0 us -> 121 us
  local copies, waits for them, and re-layouts: 0 us -> 15.8 us
  matrix products: 68.7 us -> 58.4 us
    reduce_scatter x1 -> x0, waiting for transfers between devices: 176 us -> none  [on_device(): lax.psum_scatter((weight_acc * scale).astype(jnp.bfloat16), 'dp', scatter...]
    all_to_all x0 -> x1, blocking collectives: none -> 121 us  [on_device(): lax.all_to_all(block, 'dp', split_axis=1, concat_axis=0, tiled=True)]
    all_gather x0 -> x1, waiting for transfers between devices: none -> 37.5 us  [on_device(): hidden_all = lax.all_gather(hidden, 'dp', axis=0, tiled=True)]
    dot_general x2, matrix products: 68.7 us -> 58.4 us  [the longest x1 33.4 us: on_device(): lax.dot_general(block, down_weight, (((1,), (1,)), ((), ())), preferred_e...]
    all_to_all x0 -> x1, local copies, waits for them, and re-layouts: none -> 7.98 us  [on_device(): lax.all_to_all(block, 'dp', split_axis=1, concat_axis=0, tiled=True)]
    all_gather x0 -> x1, local copies, waits for them, and re-layouts: none -> 7.84 us  [on_device(): block = lax.all_gather(out_grad, 'tensor', axis=1, tiled=True)[0]]
  transfers between devices with their start and end apart: 2 -> 2, of which waited for: 2 -> 2; matrix products, arithmetic and copies ran while one was open for 9% -> 5% of each run, Pallas kernels for 0% -> 0%
where the time goes in v1:
time: 348 us; the launch traced here: 346 us
  waiting for transfers between devices  136 us (39%)
  blocking collectives  121 us (35%)
  matrix products  58.4 us (17%)
  local copies, waits for them, and re-layouts  15.8 us (5%)
  between operations  14 us (4%)
    all_to_all x1, blocking collectives, on_device(): lax.all_to_all(block, 'dp', split_axis=1, concat_axis=0, tiled=True)  121 us
    all_gather x1, waiting for transfers between devices, on_device(): block = lax.all_gather(out_grad, 'tensor', axis=1, tiled=True)[0]  98.2 us
    all_gather x1, waiting for transfers between devices, on_device(): hidden_all = lax.all_gather(hidden, 'dp', axis=0, tiled=True)  37.5 us
    dot_general x1, matrix products, on_device(): lax.dot_general(block, down_weight, (((1,), (1,)), ((), ())), preferred_e...  33.4 us
    dot_general x1, matrix products, on_device(): jnp.einsum('tf,td->fd', hidden_all, columns, preferred_element_type=jnp.f...  25 us
    all_to_all x1, local copies, waits for them, and re-layouts, on_device(): lax.all_to_all(block, 'dp', split_axis=1, concat_axis=0, tiled=True)  7.98 us
    all_gather x1, local copies, waits for them, and re-layouts, on_device(): block = lax.all_gather(out_grad, 'tensor', axis=1, tiled=True)[0]  7.84 us
  transfers between devices with their start and end apart: 2, of which 2 were waited for; matrix products, arithmetic and copies ran while one was open for 5% of the time, Pallas kernels for 0%

profile of v1, /device:TPU:13, one launch (start us, length us, event | category | flops | bytes accessed | tf_op | source)
XLA Modules:
  0.0 345.8 jit_solution(11023457217963688195)
XLA Ops:
  7.2 0.0 all-gather.3.cloned.1.call-start
  7.2 0.7 all-gather.3.cloned.1.call-update
  7.9 0.0 all-gather.5.cloned.1.call-start
  7.9 98.2 %all-gather.3.cloned.1.call-done = bf16[1,640,4096]{2,1,0:T(8,128)(2,1)} async-done(((bf16[1,160,4096]{2,1,0:T(8,128)(2,1)}), bf16[1,640,4096]{2,1,0:T(8,128)(2,1)}) %all-gather.3.cloned.1.call-update) | async-done | bytes 5242896 | tf_op jit(solution)/shard_map/all_gather | solution.py:17
  106.2 33.4 %fusion.10 = (bf16[1,640,3584]{2,1,0:T(8,128)(2,1)}, bf16[1,640,3584]{2,1,0:T(8,128)(2,1)}, bf16[640,3584]{1,0:T(8,128)(2,1)}) fusion(bf16[1,640,3584]{2,1,0:T(8,128)(2,1)} %param.5, bf16[1,640,3584]{2,1,0:T(8,128)(2,1)} %param.6, bf16[3584,4096]{1,0:T(8,128)(2,1)} %param.7, bf16[1,640,4096]{2,1,0:T(8,128)(2,1)} %all-gather.3.cloned.1.call-done), kind=kOutput, calls=%fused_computation.17 | convolution fusion | flops 18829475840 | bytes 57540608 | tf_op jit(solution)/shard_map/dot_general | solution.py:19
  139.6 0.0 all-gather.5.cloned.1.call-update
  139.6 7.8 %copy.9 = bf16[1,640,4096]{1,2,0:T(8,128)(2,1)} copy(bf16[1,640,4096]{2,1,0:T(8,128)(2,1)} %all-gather.3.cloned.1.call-done) | data formatting | bytes 10485760 | tf_op jit(solution)/shard_map/all_gather | solution.py:17
  147.5 121.0 %all_to_all.19 = bf16[640,4,1024]{0,2,1:T(8,128)(2,1)} all-to-all(bf16[640,4,1024]{0,2,1:T(8,128)(2,1)} %bitcast.31), channel_id=1, replica_groups=mesh['groups'=2,'tensor'=4,'dp'=4] {'dp'}, dimensions={1} | all-to-all | bytes 10485760 | tf_op jit(solution)/shard_map/all_to_all | solution.py:18
  268.5 8.0 %copy.10 = bf16[4,640,1024]{2,1,0:T(8,128)(2,1)} copy(bf16[4,640,1024]{1,2,0:T(8,128)(2,1)} %bitcast.32) | data formatting | bytes 10485760 | tf_op jit(solution)/shard_map/all_to_all | solution.py:18
  276.4 37.5 %all-gather.5.cloned.1.call-done = bf16[2560,3584]{1,0:T(8,128)(2,1)} async-done(((bf16[640,3584]{1,0:T(8,128)(2,1)}), bf16[2560,3584]{1,0:T(8,128)(2,1)}) %all-gather.5.cloned.1.call-update) | async-done | bytes 18350096 | tf_op jit(solution)/shard_map/all_gather | solution.py:16
  313.9 25.0 %multiply_convert_fusion = bf16[3584,1024]{1,0:T(8,128)(2,1)} fusion(bf16[2560,3584]{1,0:T(8,128)(2,1)} %all-gather.5.cloned.1.call-done, bf16[2560,1024]{1,0:T(8,128)(2,1)} %bitcast.33), kind=kOutput, calls=%fused_computation | convolution fusion | flops 18797821952 | bytes 30932992 | tf_op jit(solution)/shard_map/tf,td->fd/dot_general | solution.py:24
Async XLA Ops:
  7.2 99.0 %all-gather.3.cloned.1.call-start = ((), (), s32[]{:S(2)}) async-start(), calls=%async_computation.1 | async-start | bytes 6553600 | tf_op jit(solution)/shard_map/all_gather | solution.py:17
  7.9 306.0 %all-gather.5.cloned.1.call-start = ((), (), s32[]{:S(2)}) async-start(), calls=%async_computation.2 | async-start | bytes 22937600 | tf_op jit(solution)/shard_map/all_gather | solution.py:16
Sparse Core Ops, SparseCore 0:
  9.6 96.5 all-gather.2
  139.7 174.1 all-gather.4

commit v2 on v1

v2 whole, which is shorter than its diff:
```python
import functools
import math

import jax
import jax.numpy as jnp
from jax import lax
from jax.experimental import pallas as pl
from jax.experimental.pallas import tpu as pltpu
from jax.sharding import PartitionSpec as P

A_PIECES = 4
B_PIECES = 2
H_PIECES = 8
MESH = pl.DeviceIdType.MESH


def exchange(
    nt, nx, tile,
    og, gate, up, weight,
    hid, cols, gate_grad, up_grad,
    og_v, xb_v, hid_v,
    own_sem, a_recv, a_up, a_dn, x_send, x_recv, b_recv, b_up, b_dn,
    hx_send, hp_send, hl_sem, h_recv, hf_send, c_local, c_send, c_recv,
):
    t = lax.axis_index("tensor")
    d = lax.axis_index("dp")
    x, c = d // 2, d % 2
    mate = x * 2 + (1 - c)
    rows, width = og.shape
    tokens, hidden_width = gate.shape
    chip_cols = width // nx
    dev_cols = width // (2 * nx)
    a_cols = width // A_PIECES
    b_cols = chip_cols // B_PIECES
    h_rows = tokens // H_PIECES
    has_up, has_dn = t < nt - 1, t > 0

    def span(i, size):
        return pl.ds(pl.multiple_of(i * size, size), size)

    def remote(src, dst, send, recv, **where):
        return pltpu.make_async_remote_copy(
            src_ref=src, dst_ref=dst, send_sem=send, recv_sem=recv,
            device_id=where, device_id_type=MESH,
        )

    def other(j):
        return (x + j) % nx

    barrier = pltpu.get_barrier_semaphore()

    @pl.when(has_up)
    def _():
        pl.semaphore_signal(barrier, 1, device_id={"tensor": t + 1}, device_id_type=MESH)

    @pl.when(has_dn)
    def _():
        pl.semaphore_signal(barrier, 1, device_id={"tensor": t - 1}, device_id_type=MESH)

    pl.semaphore_signal(barrier, 1, device_id={"dp": mate}, device_id_type=MESH)
    for j in range(1, nx):
        pl.semaphore_signal(barrier, 1, device_id={"dp": other(j) * 2 + c}, device_id_type=MESH)
    inner = jnp.logical_and(has_up, has_dn)

    @pl.when(inner)
    def _():
        pl.semaphore_wait(barrier, nx + 2)

    @pl.when(jnp.logical_not(inner))
    def _():
        pl.semaphore_wait(barrier, nx + 1)

    def a_copy(src, o, p, to, sems):
        return remote(src, og_v.at[o, :, span(p, a_cols)], sems.at[o, p], a_recv.at[o, p], tensor=to)

    def a_fwd(o, p, to, sems):
        return a_copy(og_v.at[o, :, span(p, a_cols)], o, p, to, sems)

    def b_fwd(o, xs, p, to, sems):
        ref = xb_v.at[xs, o, :, span(p, b_cols)]
        return remote(ref, ref, sems.at[o, xs, p], b_recv.at[o, xs, p], tensor=to)

    def x_copy(j):
        xo = other(j)
        return remote(
            og.at[:, span(xo, chip_cols)], xb_v.at[x, t], x_send.at[j], x_recv.at[x], dp=xo * 2 + c
        )

    own = pltpu.make_async_copy(og, og_v.at[t], own_sem)
    own.start()
    for p in range(A_PIECES):
        @pl.when(has_up)
        def _():
            a_copy(og.at[:, span(p, a_cols)], t, p, t + 1, a_up).start()

        @pl.when(has_dn)
        def _():
            a_copy(og.at[:, span(p, a_cols)], t, p, t - 1, a_dn).start()
    for j in range(1, nx):
        x_copy(j).start()

    def h_to(src, owner, i, sem, to):
        return remote(src, hid.at[owner, span(i, h_rows)], sem, h_recv.at[owner, i], dp=to)

    def h_own(i):
        src = hid_v.at[span(i, h_rows)]
        out = [h_to(src, d, i, hx_send.at[j, i], other(j) * 2 + c) for j in range(1, nx)]
        out.append(h_to(src, d, i, hp_send.at[i], mate))
        out.append(pltpu.make_async_copy(src, hid.at[d, span(i, h_rows)], hl_sem.at[i]))
        return out

    def h_fwd(j, i):
        owner = other(j) * 2 + c
        return h_to(hid.at[owner, span(i, h_rows)], owner, i, hf_send.at[j, i], mate)

    def hidden_step(gate_t, up_t):
        i = pl.program_id(0)
        g = gate_t[...].astype(jnp.float32)
        u = up_t[...].astype(jnp.float32)
        hid_v[span(i, h_rows), :] = (g * jax.nn.sigmoid(g) * u).astype(jnp.bfloat16)
        for copy in h_own(i):
            copy.start()

    row_spec = pl.BlockSpec((h_rows, hidden_width), lambda i: (i, 0))
    pltpu.emit_pipeline(hidden_step, grid=(H_PIECES,), in_specs=[row_spec, row_spec])(gate, up)

    @pl.loop(0, (nt - 1) * A_PIECES)
    def _(e):
        k, p = e // A_PIECES + 1, e % A_PIECES

        @pl.when(t - k >= 0)
        def _():
            a_fwd(t - k, p, t + 1, a_up).wait_recv()

            @pl.when(has_up)
            def _():
                a_fwd(t - k, p, t + 1, a_up).start()

        @pl.when(t + k < nt)
        def _():
            a_fwd(t + k, p, t - 1, a_dn).wait_recv()

            @pl.when(has_dn)
            def _():
                a_fwd(t + k, p, t - 1, a_dn).start()

    own.wait()
    for j in range(1, nx):
        xs = other(j)
        remote(xb_v.at[xs, t], xb_v.at[xs, t], x_send.at[j], x_recv.at[xs], dp=mate).wait_recv()
        for p in range(B_PIECES):
            @pl.when(has_up)
            def _():
                b_fwd(t, xs, p, t + 1, b_up).start()

            @pl.when(has_dn)
            def _():
                b_fwd(t, xs, p, t - 1, b_dn).start()

    def c_copies(owner, xs, ref, mine, theirs):
        return (
            pltpu.make_async_copy(ref.at[:, :, span(mine, dev_cols)], cols.at[owner], c_local.at[xs]),
            remote(ref.at[:, :, span(theirs, dev_cols)], cols.at[owner], c_send.at[xs], c_recv.at[owner], dp=mate),
        )

    for copy in c_copies(d, x, og_v, d, mate):
        copy.start()

    b_events = (nt - 1) * (nx - 1) * B_PIECES
    h_events = (nx - 1) * H_PIECES
    steps = hidden_width // tile
    per_step = -(-(b_events + h_events) // steps)

    def event(e):
        @pl.when(e < b_events)
        def _():
            k = e // ((nx - 1) * B_PIECES) + 1
            q = e % ((nx - 1) * B_PIECES)
            xs, p = other(q // B_PIECES + 1), q % B_PIECES

            @pl.when(t - k >= 0)
            def _():
                b_fwd(t - k, xs, p, t + 1, b_up).wait_recv()

                @pl.when(has_up)
                def _():
                    b_fwd(t - k, xs, p, t + 1, b_up).start()

            @pl.when(t + k < nt)
            def _():
                b_fwd(t + k, xs, p, t - 1, b_dn).wait_recv()

                @pl.when(has_dn)
                def _():
                    b_fwd(t + k, xs, p, t - 1, b_dn).start()

        @pl.when(jnp.logical_and(e >= b_events, e < b_events + h_events))
        def _():
            f = e - b_events
            h_fwd(f % (nx - 1) + 1, f // (nx - 1)).wait_recv()
            h_fwd(f % (nx - 1) + 1, f // (nx - 1)).start()

    def grad_step(w_t, gate_t, up_t, gg_t, ug_t):
        i = pl.program_id(0)
        block = og_v[...].reshape(nt * rows, width)
        grad = lax.dot_general(
            block, w_t[...], (((1,), (1,)), ((), ())), preferred_element_type=jnp.float32
        )
        g = gate_t[...].astype(jnp.float32)
        u = up_t[...].astype(jnp.float32)
        sig = jax.nn.sigmoid(g)
        gg_t[...] = (grad * u * sig * (1.0 + g * (1.0 - sig))).astype(jnp.bfloat16)
        ug_t[...] = (grad * (g * sig)).astype(jnp.bfloat16)
        for s in range(per_step):
            event(i * per_step + s)

    tile_spec = pl.BlockSpec((tokens, tile), lambda i: (0, i))
    pltpu.emit_pipeline(
        grad_step,
        grid=(steps,),
        in_specs=[pl.BlockSpec((tile, width), lambda i: (i, 0)), tile_spec, tile_spec],
        out_specs=[tile_spec, tile_spec],
    )(weight, gate, up, gate_grad, up_grad)

    for j in range(1, nx):
        xs = other(j)
        for copy in c_copies(xs * 2 + c, xs, xb_v.at[xs], c, 1 - c):
            copy.start()

    for j in range(nx):
        xs = other(j)
        local, sent = c_copies(xs * 2 + c, xs, xb_v.at[xs], c, 1 - c)
        local.wait()
        sent.wait_send()
        c_copies(xs * 2 + 1 - c, xs, xb_v.at[xs], c, 1 - c)[1].wait_recv()
    for j in range(1, nx):
        x_copy(j).wait_send()

    @pl.loop(0, H_PIECES)
    def _(i):
        *sent, local = h_own(i)
        for copy in sent:
            copy.wait_send()
        local.wait()
        for j in range(nx):
            owner = other(j) * 2 + 1 - c
            h_to(hid_v.at[span(i, h_rows)], owner, i, hp_send.at[i], mate).wait_recv()
        for j in range(1, nx):
            h_fwd(j, i).wait_send()

    @pl.loop(0, nt)
    def _(o):
        @pl.when(jnp.logical_and(has_up, o <= t))
        def _():
            for p in range(A_PIECES):
                a_fwd(o, p, t + 1, a_up).wait_send()
            for j in range(1, nx):
                for p in range(B_PIECES):
                    b_fwd(o, other(j), p, t + 1, b_up).wait_send()

        @pl.when(jnp.logical_and(has_dn, o >= t))
        def _():
            for p in range(A_PIECES):
                a_fwd(o, p, t - 1, a_dn).wait_send()
            for j in range(1, nx):
                for p in range(B_PIECES):
                    b_fwd(o, other(j), p, t - 1, b_dn).wait_send()


def on_device(out_grad, gate_pre, up_pre, down_weight):
    nt, dp = lax.axis_size("tensor"), lax.axis_size("dp")
    nx = dp // 2
    _, rows, width = out_grad.shape
    _, tokens, hidden_width = gate_pre.shape
    tile = 256 if hidden_width % 256 == 0 else 128
    bf16 = jnp.bfloat16
    dma = pltpu.SemaphoreType.DMA
    any_spec = pl.BlockSpec(memory_space=pl.ANY)
    hid, cols, gate_grad, up_grad = pl.pallas_call(
        functools.partial(exchange, nt, nx, tile),
        out_shape=(
            jax.ShapeDtypeStruct((dp, tokens, hidden_width), bf16),
            jax.ShapeDtypeStruct((dp, nt, rows, width // dp), bf16),
            jax.ShapeDtypeStruct((tokens, hidden_width), bf16),
            jax.ShapeDtypeStruct((tokens, hidden_width), bf16),
        ),
        in_specs=[any_spec] * 4,
        out_specs=[any_spec] * 4,
        scratch_shapes=[
            pltpu.VMEM((nt, rows, width), bf16),
            pltpu.VMEM((nx, nt, rows, width // nx), bf16),
            pltpu.VMEM((tokens, hidden_width), bf16),
            dma,
            dma((nt, A_PIECES)),
            dma((nt, A_PIECES)),
            dma((nt, A_PIECES)),
            dma((nx,)),
            dma((nx,)),
            dma((nt, nx, B_PIECES)),
            dma((nt, nx, B_PIECES)),
            dma((nt, nx, B_PIECES)),
            dma((nx, H_PIECES)),
            dma((H_PIECES,)),
            dma((H_PIECES,)),
            dma((dp, H_PIECES)),
            dma((nx, H_PIECES)),
            dma((nx,)),
            dma((nx,)),
            dma((dp,)),
        ],
        compiler_params=pltpu.CompilerParams(
            collective_id=0, has_side_effects=True, vmem_limit_bytes=56 * 2**20
        ),
    )(out_grad[0], gate_pre[0], up_pre[0], down_weight)
    scale = 1.0 / math.sqrt(tokens * dp)
    total = jnp.einsum(
        "tf,td->fd",
        hid.reshape(dp * tokens, hidden_width),
        cols.reshape(dp * tokens, width // dp),
        preferred_element_type=jnp.float32,
    )
    down_grad = (total * scale).astype(bf16)
    return (gate_grad[None], up_grad[None], down_grad)


def solution(mesh):
    return jax.shard_map(
        on_device,
        mesh=mesh,
        in_specs=(
            P("dp", ("groups", "tensor"), None),
            P("dp", "groups", "tensor"),
            P("dp", "groups", "tensor"),
            P("tensor", None),
        ),
        out_specs=(
            P("dp", "groups", "tensor"),
            P("dp", "groups", "tensor"),
            P(("groups", "tensor"), "dp"),
        ),
        check_vma=False,
    )
```

time: 348 us -> 185 us (0.53)
  the two profiles are of different devices: /device:TPU:13 before, /device:TPU:0 now
where the time goes in v2:
time: 185 us; the launch traced here: 184 us
  Pallas kernels  152 us (82%)
  matrix products  25.2 us (14%)
  local copies, waits for them, and re-layouts  6.1 us (3%)
    pallas_call x1, Pallas kernels, on_device(): pl.pallas_call(functools.partial(exchange, nt, nx, tile), out_shape=(jax....  152 us
    dot_general x1, matrix products, on_device(): jnp.einsum('tf,td->fd', hid.reshape(dp * tokens, hidden_width), cols.resh...  25.2 us
    unnamed x6, local copies, waits for them, and re-layouts  6.1 us

profile of v2, /device:TPU:0, one launch (start us, length us, event | category | flops | bytes accessed | tf_op | source)
XLA Modules:
  0.0 183.9 jit_solution(5523395826645096443)
XLA Ops:
  0.6 152.0 %shard_map.67 = (bf16[4,640,3584]{2,1,0:T(8,128)(2,1)}, bf16[4,4,160,1024]{3,2,1,0:T(8,128)(2,1)}, bf16[640,3584]{1,0:T(8,128)(2,1)}, bf16[640,3584]{1,0:T(8,128)(2,1)}) custom-call(bf16[160,4096]{1,0:T(8,128)(2,1)} %bitcast.13, bf16[640,3584]{1,0:T(8,128)(2,1)} %bitcast.9, bf16[640,3584]{1,0:T(8,128)(2,1)} %bitcast.10, bf16[3584,4096]{1,0:T(8,128)(2,1)} %weight.1), custom_call_target="tpu_custom_call" | custom-call | tf_op jit(solution)/shard_map/pallas_call | solution.py:279
  152.6 0.0 copy-start.1
  152.7 25.2 %multiply_convert_fusion = bf16[3584,1024]{1,0:T(8,128)(2,1)} fusion(bf16[2560,3584]{1,0:T(8,128)(2,1)} %bitcast.14, bf16[2560,1024]{1,0:T(8,128)(2,1)} %bitcast.15), kind=kOutput, calls=%fused_computation | convolution fusion | flops 18797821952 | bytes 30932992 | tf_op jit(solution)/shard_map/tf,td->fd/dot_general | solution.py:316
  177.8 0.0 copy-done.1
  177.8 0.0 copy-start
  177.8 2.3 %copy.9 = bf16[1,640,3584]{2,1,0:T(8,128)(2,1)} copy(bf16[1,640,3584]{2,1,0:T(8,128)(2,1)S(1)} %bitcast.12) | data formatting | bytes 9175040
  180.1 1.6 copy-done
  181.8 2.1 %copy.10 = bf16[1,640,3584]{2,1,0:T(8,128)(2,1)} copy(bf16[1,640,3584]{2,1,0:T(8,128)(2,1)S(1)} %bitcast.11) | data formatting | bytes 9175040
Async XLA Ops:
  152.6 25.2 %copy-start.1 = (bf16[640,3584]{1,0:T(8,128)(2,1)S(1)}, bf16[640,3584]{1,0:T(8,128)(2,1)}, u32[]{:S(2)}) copy-start(bf16[640,3584]{1,0:T(8,128)(2,1)} %get-tuple-element.7) | copy-start | bytes 13762564
  177.8 4.0 %copy-start = (bf16[640,3584]{1,0:T(8,128)(2,1)S(1)}, bf16[640,3584]{1,0:T(8,128)(2,1)}, u32[]{:S(2)}) copy-start(bf16[640,3584]{1,0:T(8,128)(2,1)} %get-tuple-element.8) | copy-start | bytes 13762564

commit v3 on v2

--- a/solution.py
+++ b/solution.py
@@ -17,10 +17,11 @@
 def exchange(
     nt, nx, tile,
     og, gate, up, weight,
-    hid, cols, gate_grad, up_grad,
+    hid_own, hid_far, cols_own, cols_far, partial, gate_grad, up_grad,
     og_v, xb_v, hid_v,
     own_sem, a_recv, a_up, a_dn, x_send, x_recv, b_recv, b_up, b_dn,
-    hx_send, hp_send, hl_sem, h_recv, hf_send, c_local, c_send, c_recv,
+    hx_send, hp_send, hl_sem, ho_recv, hf_recv, hf_send,
+    c_local, c_send, c_recv, f_local, f_send, f_recv,
 ):
     t = lax.axis_index("tensor")
     d = lax.axis_index("dp")
@@ -99,19 +100,29 @@
     for j in range(1, nx):
         x_copy(j).start()
 
-    def h_to(src, owner, i, sem, to):
-        return remote(src, hid.at[owner, span(i, h_rows)], sem, h_recv.at[owner, i], dp=to)
+    def far(j, core):
+        return (j - 1) * 2 + core
+
+    def h_mate(i):
+        rows_i = span(i, h_rows)
+        return remote(hid_v.at[rows_i], hid_own.at[c, rows_i], hp_send.at[i], ho_recv.at[c, i], dp=mate)
 
     def h_own(i):
-        src = hid_v.at[span(i, h_rows)]
-        out = [h_to(src, d, i, hx_send.at[j, i], other(j) * 2 + c) for j in range(1, nx)]
-        out.append(h_to(src, d, i, hp_send.at[i], mate))
-        out.append(pltpu.make_async_copy(src, hid.at[d, span(i, h_rows)], hl_sem.at[i]))
+        rows_i = span(i, h_rows)
+        out = []
+        for j in range(1, nx):
+            slot = far(nx - j, c)
+            out.append(remote(
+                hid_v.at[rows_i], hid_far.at[slot, rows_i], hx_send.at[j, i], hf_recv.at[slot, i],
+                dp=other(j) * 2 + c,
+            ))
+        out.append(h_mate(i))
+        out.append(pltpu.make_async_copy(hid_v.at[rows_i], hid_own.at[c, rows_i], hl_sem.at[i]))
         return out
 
-    def h_fwd(j, i):
-        owner = other(j) * 2 + c
-        return h_to(hid.at[owner, span(i, h_rows)], owner, i, hf_send.at[j, i], mate)
+    def h_fwd(j, i, core):
+        ref = hid_far.at[far(j, core), span(i, h_rows)]
+        return remote(ref, ref, hf_send.at[j, i], hf_recv.at[far(j, core), i], dp=mate)
 
     def hidden_step(gate_t, up_t):
         i = pl.program_id(0)
@@ -157,48 +168,85 @@
             def _():
                 b_fwd(t, xs, p, t - 1, b_dn).start()
 
-    def c_copies(owner, xs, ref, mine, theirs):
-        return (
-            pltpu.make_async_copy(ref.at[:, :, span(mine, dev_cols)], cols.at[owner], c_local.at[xs]),
-            remote(ref.at[:, :, span(theirs, dev_cols)], cols.at[owner], c_send.at[xs], c_recv.at[owner], dp=mate),
-        )
-
-    for copy in c_copies(d, x, og_v, d, mate):
-        copy.start()
+    def c_local_copy():
+        return pltpu.make_async_copy(og_v.at[:, :, span(d, dev_cols)], cols_own.at[c], c_local)
+
+    def c_mate():
+        return remote(og_v.at[:, :, span(mate, dev_cols)], cols_own.at[c], c_send, c_recv, dp=mate)
+
+    c_local_copy().start()
+    c_mate().start()
+
+    def f_local_copy(j, o):
+        return pltpu.make_async_copy(
+            xb_v.at[other(j), o, :, span(c, dev_cols)], cols_far.at[far(j, c), o], f_local.at[j, o]
+        )
+
+    def f_mate(j, o, core):
+        return remote(
+            xb_v.at[other(j), o, :, span(1 - c, dev_cols)], cols_far.at[far(j, core), o],
+            f_send.at[j, o], f_recv.at[far(j, core), o], dp=mate,
+        )
+
+    def share(j, o):
+        f_local_copy(j, o).start()
+        f_mate(j, o, c).start()
+
+    for j in range(1, nx):
+        share(j, t)
 
     b_events = (nt - 1) * (nx - 1) * B_PIECES
     h_events = (nx - 1) * H_PIECES
+    h_half = h_events // 2
     steps = hidden_width // tile
-    per_step = -(-(b_events + h_events) // steps)
-
-    def event(e):
-        @pl.when(e < b_events)
-        def _():
-            k = e // ((nx - 1) * B_PIECES) + 1
-            q = e % ((nx - 1) * B_PIECES)
-            xs, p = other(q // B_PIECES + 1), q % B_PIECES
-
-            @pl.when(t - k >= 0)
-            def _():
-                b_fwd(t - k, xs, p, t + 1, b_up).wait_recv()
-
-                @pl.when(has_up)
+
+    def b_arrive(e, only):
+        k = e // ((nx - 1) * B_PIECES) + 1
+        q = e % ((nx - 1) * B_PIECES)
+        j, p = q // B_PIECES + 1, q % B_PIECES
+        for o, live, to, onward, sems in (
+            (t - k, t - k >= 0, t + 1, has_up, b_up),
+            (t + k, t + k < nt, t - 1, has_dn, b_dn),
+        ):
+            wanted = onward if only else jnp.logical_not(onward)
+
+            @pl.when(jnp.logical_and(live, wanted))
+            def _():
+                b_fwd(o, other(j), p, to, sems).wait_recv()
+                if only:
+                    b_fwd(o, other(j), p, to, sems).start()
+
+                @pl.when(p == B_PIECES - 1)
                 def _():
-                    b_fwd(t - k, xs, p, t + 1, b_up).start()
-
-            @pl.when(t + k < nt)
-            def _():
-                b_fwd(t + k, xs, p, t - 1, b_dn).wait_recv()
-
-                @pl.when(has_dn)
-                def _():
-                    b_fwd(t + k, xs, p, t - 1, b_dn).start()
-
-        @pl.when(jnp.logical_and(e >= b_events, e < b_events + h_events))
-        def _():
-            f = e - b_events
-            h_fwd(f % (nx - 1) + 1, f // (nx - 1)).wait_recv()
-            h_fwd(f % (nx - 1) + 1, f // (nx - 1)).start()
+                    share(j, o)
+
+    def h_arrive(f):
+        h_fwd(f % (nx - 1) + 1, f // (nx - 1), c).wait_recv()
+        h_fwd(f % (nx - 1) + 1, f // (nx - 1), c).start()
+
+    def grad_events(i):
+        count = b_events + h_half
+        per_step = -(-count // steps)
+        for n in range(per_step):
+            e = i * per_step + n
+
+            @pl.when(e < b_events)
+            def _():
+                b_arrive(e, True)
+
+            @pl.when(jnp.logical_and(e >= b_events, e < count))
+            def _():
+                h_arrive(e - b_events)
+
+    def partial_events(i):
+        count = h_events - h_half
+        per_step = -(-count // steps)
+        for n in range(per_step):
+            e = i * per_step + n - (steps * per_step - count)
+
+            @pl.when(e >= 0)
+            def _():
+                h_arrive(h_half + e)
 
     def grad_step(w_t, gate_t, up_t, gg_t, ug_t):
         i = pl.program_id(0)
@@ -211,8 +259,7 @@
         sig = jax.nn.sigmoid(g)
         gg_t[...] = (grad * u * sig * (1.0 + g * (1.0 - sig))).astype(jnp.bfloat16)
         ug_t[...] = (grad * (g * sig)).astype(jnp.bfloat16)
-        for s in range(per_step):
-            event(i * per_step + s)
+        grad_events(i)
 
     tile_spec = pl.BlockSpec((tokens, tile), lambda i: (0, i))
     pltpu.emit_pipeline(
@@ -222,31 +269,55 @@
         out_specs=[tile_spec, tile_spec],
     )(weight, gate, up, gate_grad, up_grad)
 
-    for j in range(1, nx):
-        xs = other(j)
-        for copy in c_copies(xs * 2 + c, xs, xb_v.at[xs], c, 1 - c):
-            copy.start()
-
-    for j in range(nx):
-        xs = other(j)
-        local, sent = c_copies(xs * 2 + c, xs, xb_v.at[xs], c, 1 - c)
-        local.wait()
-        sent.wait_send()
-        c_copies(xs * 2 + 1 - c, xs, xb_v.at[xs], c, 1 - c)[1].wait_recv()
+    @pl.loop(0, H_PIECES)
+    def _(i):
+        h_own(i)[-1].wait()
+        rows_i = span(i, h_rows)
+        remote(
+            hid_v.at[rows_i], hid_own.at[1 - c, rows_i], hp_send.at[i], ho_recv.at[1 - c, i], dp=mate
+        ).wait_recv()
+
+    c_local_copy().wait()
+    remote(og_v.at[:, :, span(mate, dev_cols)], cols_own.at[1 - c], c_send, c_recv, dp=mate).wait_recv()
+
+    def partial_step(h_t, c_t, out_t):
+        out_t[...] = lax.dot_general(
+            h_t[...].reshape(2 * tokens, tile), c_t[...].reshape(2 * tokens, dev_cols),
+            (((0,), (0,)), ((), ())), preferred_element_type=jnp.float32,
+        )
+        partial_events(pl.program_id(0))
+
+    pltpu.emit_pipeline(
+        partial_step,
+        grid=(steps,),
+        in_specs=[
+            pl.BlockSpec((2, tokens, tile), lambda i: (0, 0, i)),
+            pl.BlockSpec((2, nt, rows, dev_cols), lambda i: (0, 0, 0, 0)),
+        ],
+        out_specs=[pl.BlockSpec((tile, dev_cols), lambda i: (i, 0))],
+    )(hid_own, cols_own, partial)
+
+    @pl.loop(0, b_events)
+    def _(e):
+        b_arrive(e, False)
+
+    c_mate().wait_send()
     for j in range(1, nx):
         x_copy(j).wait_send()
 
+        @pl.loop(0, nt)
+        def _(o):
+            f_local_copy(j, o).wait()
+            f_mate(j, o, c).wait_send()
+            f_mate(j, o, 1 - c).wait_recv()
+
     @pl.loop(0, H_PIECES)
     def _(i):
-        *sent, local = h_own(i)
-        for copy in sent:
+        for copy in h_own(i)[:-1]:
             copy.wait_send()
-        local.wait()
-        for j in range(nx):
-            owner = other(j) * 2 + 1 - c
-            h_to(hid_v.at[span(i, h_rows)], owner, i, hp_send.at[i], mate).wait_recv()
         for j in range(1, nx):
-            h_fwd(j, i).wait_send()
+            h_fwd(j, i, c).wait_send()
+            h_fwd(j, i, 1 - c).wait_recv()
 
     @pl.loop(0, nt)
     def _(o):
@@ -276,16 +347,20 @@
     bf16 = jnp.bfloat16
     dma = pltpu.SemaphoreType.DMA
     any_spec = pl.BlockSpec(memory_space=pl.ANY)
-    hid, cols, gate_grad, up_grad = pl.pallas_call(
+    far = 2 * (nx - 1)
+    hid_own, hid_far, cols_own, cols_far, partial, gate_grad, up_grad = pl.pallas_call(
         functools.partial(exchange, nt, nx, tile),
         out_shape=(
-            jax.ShapeDtypeStruct((dp, tokens, hidden_width), bf16),
-            jax.ShapeDtypeStruct((dp, nt, rows, width // dp), bf16),
+            jax.ShapeDtypeStruct((2, tokens, hidden_width), bf16),
+            jax.ShapeDtypeStruct((far, tokens, hidden_width), bf16),
+            jax.ShapeDtypeStruct((2, nt, rows, width // dp), bf16),
+            jax.ShapeDtypeStruct((far, nt, rows, width // dp), bf16),
+            jax.ShapeDtypeStruct((hidden_width, width // dp), jnp.float32),
             jax.ShapeDtypeStruct((tokens, hidden_width), bf16),
             jax.ShapeDtypeStruct((tokens, hidden_width), bf16),
         ),
         in_specs=[any_spec] * 4,
-        out_specs=[any_spec] * 4,
+        out_specs=[any_spec] * 7,
         scratch_shapes=[
             pltpu.VMEM((nt, rows, width), bf16),
             pltpu.VMEM((nx, nt, rows, width // nx), bf16),
@@ -302,24 +377,66 @@
             dma((nx, H_PIECES)),
             dma((H_PIECES,)),
             dma((H_PIECES,)),
-            dma((dp, H_PIECES)),
+            dma((2, H_PIECES)),
+            dma((far, H_PIECES)),
             dma((nx, H_PIECES)),
-            dma((nx,)),
-            dma((nx,)),
-            dma((dp,)),
+            dma,
+            dma,
+            dma,
+            dma((nx, nt)),
+            dma((nx, nt)),
+            dma((far, nt)),
         ],
         compiler_params=pltpu.CompilerParams(
             collective_id=0, has_side_effects=True, vmem_limit_bytes=56 * 2**20
         ),
     )(out_grad[0], gate_pre[0], up_pre[0], down_weight)
     scale = 1.0 / math.sqrt(tokens * dp)
-    total = jnp.einsum(
-        "tf,td->fd",
-        hid.reshape(dp * tokens, hidden_width),
-        cols.reshape(dp * tokens, width // dp),
-        preferred_element_type=jnp.float32,
-    )
-    down_grad = (total * scale).astype(bf16)
+    dev_cols = width // dp
+    last = hidden_width // tile - 1
+
+    def finish(h_t, c_t, part_t, gg_in, ug_in, down_t, gg_out, ug_out, sems):
+        i = pl.program_id(0)
+        copies = (
+            pltpu.make_async_copy(gg_in, gg_out, sems.at[0]),
+            pltpu.make_async_copy(ug_in, ug_out, sems.at[1]),
+        )
+
+        @pl.when(i == 0)
+        def _():
+            for copy in copies:
+                copy.start()
+
+        total = part_t[...] + lax.dot_general(
+            h_t[...].reshape(far * tokens, tile), c_t[...].reshape(far * tokens, dev_cols),
+            (((0,), (0,)), ((), ())), preferred_element_type=jnp.float32,
+        )
+        down_t[...] = (total * scale).astype(bf16)
+
+        @pl.when(i == last)
+        def _():
+            for copy in copies:
+                copy.wait()
+
+    down_grad, gate_grad, up_grad = pl.pallas_call(
+        finish,
+        grid=(last + 1,),
+        out_shape=(
+            jax.ShapeDtypeStruct((hidden_width, dev_cols), bf16),
+            jax.ShapeDtypeStruct((tokens, hidden_width), bf16),
+            jax.ShapeDtypeStruct((tokens, hidden_width), bf16),
+        ),
+        in_specs=[
+            pl.BlockSpec((far, tokens, tile), lambda i: (0, 0, i)),
+            pl.BlockSpec((far, nt, rows, dev_cols), lambda i: (0, 0, 0, 0)),
+            pl.BlockSpec((tile, dev_cols), lambda i: (i, 0)),
+            any_spec,
+            any_spec,
+        ],
+        out_specs=[pl.BlockSpec((tile, dev_cols), lambda i: (i, 0)), any_spec, any_spec],
+        scratch_shapes=[dma((2,))],
+        compiler_params=pltpu.CompilerParams(vmem_limit_bytes=48 * 2**20),
+    )(hid_far, cols_far, partial, gate_grad, up_grad)
     return (gate_grad[None], up_grad[None], down_grad)
 
 

time: 185 us -> 441 us (2.38)
  the two profiles are of different devices: /device:TPU:0 before, /device:TPU:13 now
where the time goes in v3:
time: 441 us; the launch traced here: 439 us
  Pallas kernels  437 us (99%)
    pallas_call x1, Pallas kernels, on_device(): pl.pallas_call(finish, grid=(last + 1,), out_shape=(jax.ShapeDtypeStruct(...  281 us
    pallas_call x1, Pallas kernels, on_device(): pl.pallas_call(functools.partial(exchange, nt, nx, tile), out_shape=(jax....  155 us

profile of v3, /device:TPU:13, one launch (start us, length us, event | category | flops | bytes accessed | tf_op | source)
XLA Modules:
  0.0 438.9 jit_solution(4341735538528769351)
XLA Ops:
  0.6 155.2 %shard_map.67 = (bf16[2,640,3584]{2,1,0:T(8,128)(2,1)}, bf16[2,640,3584]{2,1,0:T(8,128)(2,1)}, bf16[2,4,160,1024]{3,2,1,0:T(8,128)(2,1)}, bf16[2,4,160,1024]{3,2...) custom-call(bf16[160,4096]{1,0:T(8,128)(2,1)} %bitcast.7, ...), custom_call_target="tpu_custom_call" | custom-call | tf_op jit(solution)/shard_map/pallas_call | solution.py:351
  155.9 0.0 copy-start
  155.9 1.7 copy-done
  157.6 281.3 %shard_map.68 = (bf16[3584,1024]{1,0:T(8,128)(2,1)}, bf16[640,3584]{1,0:T(8,128)(2,1)}, bf16[640,3584]{1,0:T(8,128)(2,1)}) custom-call(bf16[2,640,3584]{2,1,0:T(8,128)(2,1)} %get-tuple-element.11.h_t, bf16[2,4,160,1024]{3,2,1,0:T(8,128)(2,1)S(1)} %copy-done, f32[3584,1024]{1,0:T(8,128)} %get-tuple-element.13.part_t, ...), custom_call_target="tpu_custom_call" | custom-call | tf_op jit(solution)/shard_map/pallas_call | solution.py:421
Async XLA Ops:
  155.9 1.7 copy-start

commit v4 on v3

--- a/solution.py
+++ b/solution.py
@@ -284,7 +284,7 @@
         out_t[...] = lax.dot_general(
             h_t[...].reshape(2 * tokens, tile), c_t[...].reshape(2 * tokens, dev_cols),
             (((0,), (0,)), ((), ())), preferred_element_type=jnp.float32,
-        )
+        ).astype(jnp.bfloat16)
         partial_events(pl.program_id(0))
 
     pltpu.emit_pipeline(
@@ -355,7 +355,7 @@
             jax.ShapeDtypeStruct((far, tokens, hidden_width), bf16),
             jax.ShapeDtypeStruct((2, nt, rows, width // dp), bf16),
             jax.ShapeDtypeStruct((far, nt, rows, width // dp), bf16),
-            jax.ShapeDtypeStruct((hidden_width, width // dp), jnp.float32),
+            jax.ShapeDtypeStruct((hidden_width, width // dp), bf16),
             jax.ShapeDtypeStruct((tokens, hidden_width), bf16),
             jax.ShapeDtypeStruct((tokens, hidden_width), bf16),
         ),
@@ -392,51 +392,13 @@
         ),
     )(out_grad[0], gate_pre[0], up_pre[0], down_weight)
     scale = 1.0 / math.sqrt(tokens * dp)
-    dev_cols = width // dp
-    last = hidden_width // tile - 1
-
-    def finish(h_t, c_t, part_t, gg_in, ug_in, down_t, gg_out, ug_out, sems):
-        i = pl.program_id(0)
-        copies = (
-            pltpu.make_async_copy(gg_in, gg_out, sems.at[0]),
-            pltpu.make_async_copy(ug_in, ug_out, sems.at[1]),
-        )
-
-        @pl.when(i == 0)
-        def _():
-            for copy in copies:
-                copy.start()
-
-        total = part_t[...] + lax.dot_general(
-            h_t[...].reshape(far * tokens, tile), c_t[...].reshape(far * tokens, dev_cols),
-            (((0,), (0,)), ((), ())), preferred_element_type=jnp.float32,
-        )
-        down_t[...] = (total * scale).astype(bf16)
-
-        @pl.when(i == last)
-        def _():
-            for copy in copies:
-                copy.wait()
-
-    down_grad, gate_grad, up_grad = pl.pallas_call(
-        finish,
-        grid=(last + 1,),
-        out_shape=(
-            jax.ShapeDtypeStruct((hidden_width, dev_cols), bf16),
-            jax.ShapeDtypeStruct((tokens, hidden_width), bf16),
-            jax.ShapeDtypeStruct((tokens, hidden_width), bf16),
-        ),
-        in_specs=[
-            pl.BlockSpec((far, tokens, tile), lambda i: (0, 0, i)),
-            pl.BlockSpec((far, nt, rows, dev_cols), lambda i: (0, 0, 0, 0)),
-            pl.BlockSpec((tile, dev_cols), lambda i: (i, 0)),
-            any_spec,
-            any_spec,
-        ],
-        out_specs=[pl.BlockSpec((tile, dev_cols), lambda i: (i, 0)), any_spec, any_spec],
-        scratch_shapes=[dma((2,))],
-        compiler_params=pltpu.CompilerParams(vmem_limit_bytes=48 * 2**20),
-    )(hid_far, cols_far, partial, gate_grad, up_grad)
+    total = partial.astype(jnp.float32) + jnp.einsum(
+        "tf,td->fd",
+        hid_far.reshape(far * tokens, hidden_width),
+        cols_far.reshape(far * tokens, width // dp),
+        preferred_element_type=jnp.float32,
+    )
+    down_grad = (total * scale).astype(bf16)
     return (gate_grad[None], up_grad[None], down_grad)
 
 

time: 441 us -> 179 us (0.41)
  Pallas kernels: 437 us -> 154 us
  matrix products: 0 us -> 16.5 us
    pallas_call x1 -> x0, Pallas kernels: 281 us -> none  [on_device(): pl.pallas_call(finish, grid=(last + 1,), out_shape=(jax.ShapeDtypeStruct(...]
    dot_general x0 -> x1, matrix products: none -> 16.5 us  [on_device(): jnp.einsum('tf,td->fd', hid_far.reshape(far * tokens, hidden_width), cols...]
where the time goes in v4:
time: 179 us; the launch traced here: 177 us
  Pallas kernels  154 us (86%)
  matrix products  16.5 us (9%)
  local copies, waits for them, and re-layouts  6.1 us (3%)
    pallas_call x1, Pallas kernels, on_device(): pl.pallas_call(functools.partial(exchange, nt, nx, tile), out_shape=(jax....  154 us
    dot_general x1, matrix products, on_device(): jnp.einsum('tf,td->fd', hid_far.reshape(far * tokens, hidden_width), cols...  16.5 us
    unnamed x6, local copies, waits for them, and re-layouts  6.1 us

profile of v4, /device:TPU:13, one launch (start us, length us, event | category | flops | bytes accessed | tf_op | source)
XLA Modules:
  0.0 177.3 jit_solution(1425575820574819491)
XLA Ops:
  0.6 154.1 %shard_map.67 = (bf16[2,640,3584]{2,1,0:T(8,128)(2,1)}, bf16[2,640,3584]{2,1,0:T(8,128)(2,1)}, bf16[2,4,160,1024]{3,2,1,0:T(8,128)(2,1)}, bf16[2,4,160,1024]{3,2...) custom-call(bf16[160,4096]{1,0:T(8,128)(2,1)} %bitcast.13, ...), custom_call_target="tpu_custom_call" | custom-call | tf_op jit(solution)/shard_map/pallas_call | solution.py:351
  154.8 0.0 copy-start.1
  154.8 16.5 %multiply_convert_fusion = bf16[3584,1024]{1,0:T(8,128)(2,1)} fusion(bf16[3584,1024]{1,0:T(8,128)(2,1)} %get-tuple-element.10, bf16[1280,3584]{1,0:T(8,128)(2,1)} %bitcast.14, bf16[1280,1024]{1,0:T(8,128)(2,1)} %bitcast.15), kind=kOutput, calls=%fused_computation | convolution fusion | flops 9409921024 | bytes 26476544 | tf_op jit(solution)/shard_map/tf,td->fd/dot_general | solution.py:395
  171.2 0.0 copy-done.1
  171.2 0.0 copy-start
  171.2 2.3 %copy.9 = bf16[1,640,3584]{2,1,0:T(8,128)(2,1)} copy(bf16[1,640,3584]{2,1,0:T(8,128)(2,1)S(1)} %bitcast.12) | data formatting | bytes 9175040
  173.6 1.6 copy-done
  175.2 2.1 %copy.10 = bf16[1,640,3584]{2,1,0:T(8,128)(2,1)} copy(bf16[1,640,3584]{2,1,0:T(8,128)(2,1)S(1)} %bitcast.11) | data formatting | bytes 9175040
Async XLA Ops:
  154.8 16.5 %copy-start.1 = (bf16[640,3584]{1,0:T(8,128)(2,1)S(1)}, bf16[640,3584]{1,0:T(8,128)(2,1)}, u32[]{:S(2)}) copy-start(bf16[640,3584]{1,0:T(8,128)(2,1)} %get-tuple-element.8) | copy-start | bytes 13762564
  171.2 4.0 %copy-start = (bf16[640,3584]{1,0:T(8,128)(2,1)S(1)}, bf16[640,3584]{1,0:T(8,128)(2,1)}, u32[]{:S(2)}) copy-start(bf16[640,3584]{1,0:T(8,128)(2,1)} %get-tuple-element.9) | copy-start | bytes 13762564
